TPU v7x, 32 devices: a whole 2x2x4 slice. The times are simulated.
32 devices in a mesh: row: 8 (over y, x, core), col: 4 (over z).
Axes of the slice: x: 2, y: 2, z: 4, core: 2. Of those that a mesh axis runs over, the one named last changes fastest.
Arguments:
- dual_ops: float32 [8, 4, 2048, 2048], P('row', 'col'), as said below
- basis: float32 [8, 4, 4, 64, 512], P('row', 'col'), may hold values from -0.125 to 0.125
- coarse_inverse: float32 [2048, 2048], P('row', 'col')
- gap_rhs: float32 [8, 4, 4, 32, 512], P('row', 'col'), may hold values from -6 to 6
- coarse_rhs: float32 [8, 4, 32, 64], P('row', 'col'), may hold values from -6 to 6
- contact_mask: int32 [8, 4, 4, 512], P('row', 'col'), may hold values 0 or 1
Outputs:
- multipliers: float32 [8, 4, 4, 32, 512], P('row', 'col')
- projected_grad: float32 [8, 4, 4, 32, 512], P('row', 'col')
Inputs may be any that keep to these rules, and one draw needn't show every extreme that they name: `dual_ops`: each subdomain's dual operator is symmetric and positive definite.
All inputs are finite; a program needn't handle non-finite values. No bound on the sum of `contact_mask` on one device may be relied on, other than what follows from the above.
Results may differ from a plain program's by a relative error of at most 0.00025.
Values sent between devices are 32-bit elements; how exact they have to be, the bound alone decides.
A program may use at most 128 MiB of HBM per device.

v0:
```python
import jax
import jax.numpy as jnp
from jax import lax
from jax.sharding import PartitionSpec as P

MDEV = 64
ITERS = 6
HIGH = lax.Precision.HIGHEST


def padded(block, sides, width):
    for axis, dim in sides:
        count = lax.axis_size(axis)
        forward = [(i, i + 1) for i in range(count - 1)]
        backward = [(target, source) for source, target in forward]
        low = lax.ppermute(
            lax.slice_in_dim(block, block.shape[dim] - width, None, axis=dim), axis, forward
        )
        high = lax.ppermute(lax.slice_in_dim(block, 0, width, axis=dim), axis, backward)
        block = jnp.concatenate([low, block, high], axis=dim)
    return block


def neighbour_faces(values):
    rows_padded = padded(values[0:2], (("row", 0),), 1)
    cols_padded = padded(values[2:4], (("col", 0),), 1)
    return jnp.stack([rows_padded[0], rows_padded[3], cols_padded[0], cols_padded[3]], axis=0)


def shards(dual_ops, basis, coarse_inverse, gap_rhs, coarse_rhs, contact_mask):
    face_len = gap_rhs.shape[-1]
    blocks = dual_ops[0, 0].reshape(4, face_len, 4, face_len)
    local_basis = basis[0, 0]
    row_idx = lax.axis_index("row")
    col_idx = lax.axis_index("col")
    n_rows = lax.axis_size("row")
    n_cols = lax.axis_size("col")
    has_nb = jnp.stack([row_idx > 0, row_idx < n_rows - 1, col_idx > 0, col_idx < n_cols - 1])
    weight = jnp.where(has_nb, 0.5, 1.0).astype(jnp.float32)[:, None, None]
    contact = jnp.logical_and(contact_mask[0, 0] == 1, jnp.logical_not(has_nb)[:, None])[:, None, :]

    def apply_dual(vector):
        return jnp.einsum("gjfi,fki->gkj", blocks, vector, precision=HIGH)

    def coarse(coef):
        gathered = lax.all_gather(coef, "row", axis=1, tiled=True)
        partial_amps = lax.dot_general(
            gathered,
            coarse_inverse,
            (((1,), (1,)), ((), ())),
            precision=HIGH,
            preferred_element_type=jnp.float32,
        )
        summed = lax.psum(partial_amps, "col")
        return lax.dynamic_slice_in_dim(summed, col_idx * MDEV, MDEV, 1)

    def expand_sum(amps):
        own = jnp.einsum("fji,kj->fki", local_basis, amps, precision=HIGH)
        return own + neighbour_faces(own)

    local_rhs = gap_rhs[0, 0]
    dvec = local_rhs + neighbour_faces(local_rhs)
    multipliers = expand_sum(coarse(coarse_rhs[0, 0]))
    projected = jnp.zeros_like(multipliers)
    for step in range(ITERS):
        applied = apply_dual(multipliers)
        grad = applied + neighbour_faces(applied) - dvec
        projected = grad - expand_sum(
            coarse(jnp.einsum("fji,fki->kj", local_basis, grad, precision=HIGH))
        )
        image = apply_dual(projected)
        numer = jnp.sum(weight * grad * projected, axis=(0, 2))
        denom = jnp.sum(projected * image, axis=(0, 2))
        numer_all, denom_all = lax.psum((numer, denom), ("row", "col"))
        ratio = numer_all / denom_all
        multipliers = multipliers - ratio[None, :, None] * projected
        multipliers = jnp.where(contact, jnp.maximum(multipliers, 0.0), multipliers)
    return (multipliers[None, None], projected[None, None])


def solution(mesh):
    return jax.shard_map(
        shards,
        mesh=mesh,
        in_specs=(
            P("row", "col", None, None),
            P("row", "col", None, None, None),
            P("row", "col"),
            P("row", "col", None, None, None),
            P("row", "col", None, None),
            P("row", "col", None, None),
        ),
        out_specs=(P("row", "col", None, None, None), P("row", "col", None, None, None)),
        check_vma=False,
    )
```

profile of v0, /device:TPU:0, one launch (start us, length us, event | category | flops | bytes accessed | tf_op | source)
XLA Modules:
  0.0 938.7 jit_solution(12016818391664905516)
XLA Ops:
  13.9 19.3 %psum.133 = f32[32,256]{1,0:T(8,128)S(1)} all-reduce(f32[32,256]{1,0:T(8,128)S(1)} %fusion.178), channel_id=1, replica_groups=mesh['row'=8,'col'=4] {'col'}, use_global_device_ids=true, to_apply=%region_0.1 | all-reduce | flops 8192 | bytes 65536 | tf_op jit(solution)/shard_map/psum | solution.py:54
  47.3 20.4 %reshape_squeeze.3 = f32[4,512,4,512]{3,2,1,0:T(4,128)} reshape(f32[1,1,2048,2048]{3,2,1,0:T(8,128)} %param.6) | data formatting | bytes 33554432 | tf_op jit(solution)/shard_map/reshape;squeeze | solution.py:32
  75.3 24.6 %fusion.24 = f32[4,32,512]{2,1,0:T(8,128)S(1)} fusion(f32[4,512,4,512]{3,2,1,0:T(4,128)} %reshape_squeeze.3, f32[4,32,512]{2,1,0:T(8,128)S(1)} %convolution_bitcast_fusion.6, f32[1,32,512]{2,1,0:T(8,128)S(1)} %collective-permute-done.3, f32[1,32,512]{2,1,0:T(8,128)S(1)} %collective-permute-done.2, f32[1,32,512]{2,1,0:T(8,128)S(1)} %collective-permute-done.1, ...), kind=kOutput, calls=%fused_computation.24 | convolution fusion | flops 1610874880 | bytes 17563648 | tf_op jit(solution)/shard_map/gjfi,fki->gkj/dot_general | solution.py:43
  156.7 22.3 %fusion.78 = f32[32]{0:T(128)S(1)} fusion(f32[4,32,512]{2,1,0:T(8,128)S(1)} %get-tuple-element.27, f32[4,512,4,512]{3,2,1,0:T(4,128)} %reshape_squeeze.3), kind=kOutput, calls=%fused_computation.49 | convolution fusion | flops 1610743808 | bytes 17039488 | tf_op jit(solution)/shard_map/gjfi,fki->gkj/dot_general | solution.py:43
  179.0 41.7 %all-reduce.5 = (f32[32]{0:T(128)S(1)}, f32[32]{0:T(128)S(1)}) all-reduce(f32[32]{0:T(128)S(1)} %get-tuple-element.26, f32[32]{0:T(128)S(1)} %fusion.78), channel_id=1, replica_groups=mesh['row'=8,'col'=4] {'row','col'}, use_global_device_ids=true, to_apply=%region_3.4 | all-reduce | flops 64 | bytes 512 | tf_op jit(solution)/shard_map/psum | solution.py:74
  220.8 24.6 %fusion.30 = f32[4,32,512]{2,1,0:T(8,128)S(1)} fusion(f32[4,512,4,512]{3,2,1,0:T(4,128)} %reshape_squeeze.3, f32[4,32,512]{2,1,0:T(8,128)S(1)} %maximum_select_fusion.5), kind=kOutput, calls=%fused_computation.26 | convolution fusion | flops 1610612736 | bytes 17301504 | tf_op jit(solution)/shard_map/gjfi,fki->gkj/dot_general | solution.py:43
  270.4 17.6 %psum.137 = f32[32,256]{1,0:T(8,128)S(1)} all-reduce(f32[32,256]{1,0:T(8,128)S(1)} %fusion.180), channel_id=1, replica_groups=mesh['row'=8,'col'=4] {'col'}, use_global_device_ids=true, to_apply=%region_6.7 | all-reduce | flops 8192 | bytes 65536 | tf_op jit(solution)/shard_map/psum | solution.py:54
  300.3 22.3 %fusion.81 = f32[32]{0:T(128)S(1)} fusion(f32[4,32,512]{2,1,0:T(8,128)S(1)} %get-tuple-element.23, f32[4,512,4,512]{3,2,1,0:T(4,128)} %reshape_squeeze.3), kind=kOutput, calls=%fused_computation.50 | convolution fusion | flops 1610743808 | bytes 17039488 | tf_op jit(solution)/shard_map/gjfi,fki->gkj/dot_general | solution.py:43
  322.6 41.5 %all-reduce.4 = (f32[32]{0:T(128)S(1)}, f32[32]{0:T(128)S(1)}) all-reduce(f32[32]{0:T(128)S(1)} %get-tuple-element.22, f32[32]{0:T(128)S(1)} %fusion.81), channel_id=1, replica_groups=mesh['row'=8,'col'=4] {'row','col'}, use_global_device_ids=true, to_apply=%region_8.9 | all-reduce | flops 64 | bytes 512 | tf_op jit(solution)/shard_map/psum | solution.py:74
  364.1 24.4 %fusion.36 = f32[4,32,512]{2,1,0:T(8,128)S(1)} fusion(f32[4,512,4,512]{3,2,1,0:T(4,128)} %reshape_squeeze.3, f32[4,32,512]{2,1,0:T(8,128)S(1)} %maximum_select_fusion.5, f32[4,32,512]{2,1,0:T(8,128)S(1)} %get-tuple-element.23, f32[32]{0:T(128)S(1)} %div.19, pred[4,512]{1,0:T(4,128)(4,1)S(1)} %bitcast_and_fusion), kind=kOutput, calls=%fused_computation.28 | convolution fusion | flops 1610874880 | bytes 17565824 | tf_op jit(solution)/shard_map/gjfi,fki->gkj/dot_general | solution.py:43
  413.5 17.9 %psum.140 = f32[32,256]{1,0:T(8,128)S(1)} all-reduce(f32[32,256]{1,0:T(8,128)S(1)} %fusion.181), channel_id=1, replica_groups=mesh['row'=8,'col'=4] {'col'}, use_global_device_ids=true, to_apply=%region_11.12 | all-reduce | flops 8192 | bytes 65536 | tf_op jit(solution)/shard_map/psum | solution.py:54
  443.7 22.3 %fusion.84 = f32[32]{0:T(128)S(1)} fusion(f32[4,32,512]{2,1,0:T(8,128)S(1)} %get-tuple-element.21, f32[4,512,4,512]{3,2,1,0:T(4,128)} %reshape_squeeze.3), kind=kOutput, calls=%fused_computation.51 | convolution fusion | flops 1610743808 | bytes 17039488 | tf_op jit(solution)/shard_map/gjfi,fki->gkj/dot_general | solution.py:43
  465.9 41.4 %all-reduce.3 = (f32[32]{0:T(128)S(1)}, f32[32]{0:T(128)S(1)}) all-reduce(f32[32]{0:T(128)S(1)} %get-tuple-element.20, f32[32]{0:T(128)S(1)} %fusion.84), channel_id=1, replica_groups=mesh['row'=8,'col'=4] {'row','col'}, use_global_device_ids=true, to_apply=%region_13.14 | all-reduce | flops 64 | bytes 512 | tf_op jit(solution)/shard_map/psum | solution.py:74
  507.5 24.6 %fusion.42 = f32[4,32,512]{2,1,0:T(8,128)S(1)} fusion(f32[4,512,4,512]{3,2,1,0:T(4,128)} %reshape_squeeze.3, f32[4,32,512]{2,1,0:T(8,128)S(1)} %maximum_select_fusion.3), kind=kOutput, calls=%fused_computation.30 | convolution fusion | flops 1610612736 | bytes 17301504 | tf_op jit(solution)/shard_map/gjfi,fki->gkj/dot_general | solution.py:43
  557.2 17.7 %psum.143 = f32[32,256]{1,0:T(8,128)S(1)} all-reduce(f32[32,256]{1,0:T(8,128)S(1)} %fusion.182), channel_id=1, replica_groups=mesh['row'=8,'col'=4] {'col'}, use_global_device_ids=true, to_apply=%region_16.17 | all-reduce | flops 8192 | bytes 65536 | tf_op jit(solution)/shard_map/psum | solution.py:54
  587.1 22.3 %fusion.87 = f32[32]{0:T(128)S(1)} fusion(f32[4,32,512]{2,1,0:T(8,128)S(1)} %get-tuple-element.19, f32[4,512,4,512]{3,2,1,0:T(4,128)} %reshape_squeeze.3), kind=kOutput, calls=%fused_computation.52 | convolution fusion | flops 1610743808 | bytes 17039488 | tf_op jit(solution)/shard_map/gjfi,fki->gkj/dot_general | solution.py:43
  609.4 41.7 %all-reduce.2 = (f32[32]{0:T(128)S(1)}, f32[32]{0:T(128)S(1)}) all-reduce(f32[32]{0:T(128)S(1)} %get-tuple-element.18, f32[32]{0:T(128)S(1)} %fusion.87), channel_id=1, replica_groups=mesh['row'=8,'col'=4] {'row','col'}, use_global_device_ids=true, to_apply=%region_18.19 | all-reduce | flops 64 | bytes 512 | tf_op jit(solution)/shard_map/psum | solution.py:74
  651.1 24.4 %fusion.48 = f32[4,32,512]{2,1,0:T(8,128)S(1)} fusion(f32[4,512,4,512]{3,2,1,0:T(4,128)} %reshape_squeeze.3, f32[4,32,512]{2,1,0:T(8,128)S(1)} %maximum_select_fusion.3, f32[4,32,512]{2,1,0:T(8,128)S(1)} %get-tuple-element.19, f32[32]{0:T(128)S(1)} %div.21, pred[4,512]{1,0:T(4,128)(4,1)S(1)} %bitcast_and_fusion), kind=kOutput, calls=%fused_computation.32 | convolution fusion | flops 1610874880 | bytes 17565824 | tf_op jit(solution)/shard_map/gjfi,fki->gkj/dot_general | solution.py:43
  730.4 22.3 %fusion.90 = f32[32]{0:T(128)S(1)} fusion(f32[4,32,512]{2,1,0:T(8,128)S(1)} %get-tuple-element.17, f32[4,512,4,512]{3,2,1,0:T(4,128)} %reshape_squeeze.3), kind=kOutput, calls=%fused_computation.53 | convolution fusion | flops 1610743808 | bytes 17039488 | tf_op jit(solution)/shard_map/gjfi,fki->gkj/dot_general | solution.py:43
  752.7 41.5 %all-reduce.1 = (f32[32]{0:T(128)S(1)}, f32[32]{0:T(128)S(1)}) all-reduce(f32[32]{0:T(128)S(1)} %get-tuple-element.16, f32[32]{0:T(128)S(1)} %fusion.90), channel_id=1, replica_groups=mesh['row'=8,'col'=4] {'row','col'}, use_global_device_ids=true, to_apply=%region_23.24 | all-reduce | flops 64 | bytes 512 | tf_op jit(solution)/shard_map/psum | solution.py:74
  794.4 24.6 %fusion.54 = f32[4,32,512]{2,1,0:T(8,128)S(1)} fusion(f32[4,512,4,512]{3,2,1,0:T(4,128)} %reshape_squeeze.3, f32[4,32,512]{2,1,0:T(8,128)S(1)} %maximum_select_fusion.1), kind=kOutput, calls=%fused_computation.34 | convolution fusion | flops 1610612736 | bytes 17301504 | tf_op jit(solution)/shard_map/gjfi,fki->gkj/dot_general | solution.py:43
  844.0 17.7 %psum.149 = f32[32,256]{1,0:T(8,128)S(1)} all-reduce(f32[32,256]{1,0:T(8,128)S(1)} %fusion.184), channel_id=1, replica_groups=mesh['row'=8,'col'=4] {'col'}, use_global_device_ids=true, to_apply=%region_26.27 | all-reduce | flops 8192 | bytes 65536 | tf_op jit(solution)/shard_map/psum | solution.py:54
  874.0 22.4 %fusion.93 = f32[32]{0:T(128)S(1)} fusion(f32[4,32,512]{2,1,0:T(8,128)S(1)} %get-tuple-element.15, f32[4,512,4,512]{3,2,1,0:T(4,128)} %reshape_squeeze.3), kind=kOutput, calls=%fused_computation.54 | convolution fusion | flops 1610743808 | bytes 17039488 | tf_op jit(solution)/shard_map/gjfi,fki->gkj/dot_general | solution.py:43
  896.4 41.3 %all-reduce = (f32[32]{0:T(128)S(1)}, f32[32]{0:T(128)S(1)}) all-reduce(f32[32]{0:T(128)S(1)} %get-tuple-element.14, f32[32]{0:T(128)S(1)} %fusion.93), channel_id=1, replica_groups=mesh['row'=8,'col'=4] {'row','col'}, use_global_device_ids=true, to_apply=%region_28.29 | all-reduce | flops 64 | bytes 512 | tf_op jit(solution)/shard_map/psum | solution.py:74
  (203 shorter events, 296.2 us)
Async XLA Ops:
  33.6 34.2 %collective-permute-start = (f32[1,32,512]{2,1,0:T(8,128)S(1)}, f32[1,32,512]{2,1,0:T(8,128)S(1)}, u32[]{:S(2)}, u32[]{:S(2)}) collective-permute-start(f32[1,32,512]{2,1,0:T(8,128)S(1)} %get-tuple-element.82), channel_id=1, source_target_pairs={{0,4},{4,8},{8,12},{12,16},{16,20},{20,24},{24,28},{1,5},{5,9},{9,... | collective-permute-start | bytes 196616 | tf_op jit(solution)/shard_map/ppermute | solution.py:16
  34.9 34.3 %collective-permute-start.3 = (f32[1,32,512]{2,1,0:T(8,128)S(1)}, f32[1,32,512]{2,1,0:T(8,128)S(1)}, u32[]{:S(2)}, u32[]{:S(2)}) collective-permute-start(f32[1,32,512]{2,1,0:T(8,128)S(1)} %get-tuple-element.83), channel_id=1, source_target_pairs={{1,0},{2,1},{3,2},{5,4},{6,5},{7,6},{9,8},{10,9},{11,10},{13,12},{... | collective-permute-start | bytes 196616 | tf_op jit(solution)/shard_map/ppermute | solution.py:19
  36.2 34.3 %collective-permute-start.2 = (f32[1,32,512]{2,1,0:T(8,128)S(1)}, f32[1,32,512]{2,1,0:T(8,128)S(1)}, u32[]{:S(2)}, u32[]{:S(2)}) collective-permute-start(f32[1,32,512]{2,1,0:T(8,128)S(1)} %get-tuple-element.84), channel_id=1, source_target_pairs={{0,1},{1,2},{2,3},{4,5},{5,6},{6,7},{8,9},{9,10},{10,11},{12,13},{... | collective-permute-start | bytes 196616 | tf_op jit(solution)/shard_map/ppermute | solution.py:16
  40.8 34.5 %collective-permute-start.1 = (f32[1,32,512]{2,1,0:T(8,128)S(1)}, f32[1,32,512]{2,1,0:T(8,128)S(1)}, u32[]{:S(2)}, u32[]{:S(2)}) collective-permute-start(f32[1,32,512]{2,1,0:T(8,128)S(1)} %get-tuple-element.85), channel_id=1, source_target_pairs={{4,0},{8,4},{12,8},{16,12},{20,16},{24,20},{28,24},{5,1},{9,5},{13... | collective-permute-start | bytes 196616 | tf_op jit(solution)/shard_map/ppermute | solution.py:19
  43.0 60.6 %collective-permute-start.8 = (f32[1,32,512]{2,1,0:T(8,128)S(1)}, f32[1,32,512]{2,1,0:T(8,128)S(1)}, u32[]{:S(2)}, u32[]{:S(2)}) collective-permute-start(f32[1,32,512]{2,1,0:T(8,128)S(1)} %get-tuple-element.74), channel_id=1, source_target_pairs={{0,4},{4,8},{8,12},{12,16},{16,20},{20,24},{24,28},{1,5},{5,9},{9,... | collective-permute-start | bytes 196616 | tf_op jit(solution)/shard_map/ppermute | solution.py:16
  67.8 37.1 %collective-permute-start.9 = (f32[1,32,512]{2,1,0:T(8,128)S(1)}, f32[1,32,512]{2,1,0:T(8,128)S(1)}, u32[]{:S(2)}, u32[]{:S(2)}) collective-permute-start(f32[1,32,512]{2,1,0:T(8,128)S(1)} %get-tuple-element.75), channel_id=1, source_target_pairs={{4,0},{8,4},{12,8},{16,12},{20,16},{24,20},{28,24},{5,1},{9,5},{13... | collective-permute-start | bytes 196616 | tf_op jit(solution)/shard_map/ppermute | solution.py:19
  69.2 40.3 %collective-permute-start.11 = (f32[1,32,512]{2,1,0:T(8,128)S(1)}, f32[1,32,512]{2,1,0:T(8,128)S(1)}, u32[]{:S(2)}, u32[]{:S(2)}) collective-permute-start(f32[1,32,512]{2,1,0:T(8,128)S(1)} %get-tuple-element.76), channel_id=1, source_target_pairs={{1,0},{2,1},{3,2},{5,4},{6,5},{7,6},{9,8},{10,9},{11,10},{13,12},{... | collective-permute-start | bytes 196616 | tf_op jit(solution)/shard_map/ppermute | solution.py:19
  70.5 40.4 %collective-permute-start.10 = (f32[1,32,512]{2,1,0:T(8,128)S(1)}, f32[1,32,512]{2,1,0:T(8,128)S(1)}, u32[]{:S(2)}, u32[]{:S(2)}) collective-permute-start(f32[1,32,512]{2,1,0:T(8,128)S(1)} %get-tuple-element.77), channel_id=1, source_target_pairs={{0,1},{1,2},{2,3},{4,5},{5,6},{6,7},{8,9},{9,10},{10,11},{12,13},{... | collective-permute-start | bytes 196616 | tf_op jit(solution)/shard_map/ppermute | solution.py:16
  99.9 11.0 %collective-permute-start.4 = (f32[1,32,512]{2,1,0:T(8,128)S(1)}, f32[1,32,512]{2,1,0:T(8,128)S(1)}, u32[]{:S(2)}, u32[]{:S(2)}) collective-permute-start(f32[1,32,512]{2,1,0:T(8,128)S(1)} %get-tuple-element.78), channel_id=1, source_target_pairs={{0,4},{4,8},{8,12},{12,16},{16,20},{20,24},{24,28},{1,5},{5,9},{9,... | collective-permute-start | bytes 196616 | tf_op jit(solution)/shard_map/ppermute | solution.py:16
  103.6 7.3 collective-permute-start.7
  144.9 8.7 collective-permute-start.12
  146.2 7.4 collective-permute-start.15
  245.4 8.5 collective-permute-start.16
  246.7 7.2 collective-permute-start.19
  288.5 8.5 collective-permute-start.20
  388.5 8.5 collective-permute-start.24
  431.9 8.5 collective-permute-start.28
  532.1 8.5 collective-permute-start.32
  575.3 8.5 collective-permute-start.36
  675.5 8.5 collective-permute-start.40
  718.7 8.5 collective-permute-start.44
  818.9 8.5 collective-permute-start.48
  820.2 7.2 collective-permute-start.51
  862.2 8.5 collective-permute-start.52
  (37 other events, 437.7 us)
where the time goes:
time: 944 us; the launch traced here: 939 us
  blocking collectives  454 us (48%)
  matrix products  292 us (31%)
  starting transfers between devices  124 us (13%)
  waiting for transfers between devices  40.5 us (4%)
  local copies, waits for them, and re-layouts  23.6 us (2%)
    dot_general x12, matrix products, apply_dual(): return jnp.einsum('gjfi,fki->gkj', blocks, vector, precision=HIGH)  281 us
    psum x6, blocking collectives, shards(): numer_all, denom_all = lax.psum((numer, denom), ('row', 'col'))  249 us
    psum x7, blocking collectives, coarse(): summed = lax.psum(partial_amps, 'col')  124 us
    ppermute x28, starting transfers between devices, padded(): lax.ppermute(lax.slice_in_dim(block, block.shape[dim] - width, None, axis...  87.3 us
    all_gather x7, blocking collectives, coarse(): gathered = lax.all_gather(coef, 'row', axis=1, tiled=True)  80.8 us
    ppermute x28, starting transfers between devices, padded(): lax.ppermute(lax.slice_in_dim(block, 0, width, axis=dim), axis, backward)  36.5 us
    ppermute x28, waiting for transfers between devices, padded(): lax.ppermute(lax.slice_in_dim(block, 0, width, axis=dim), axis, backward)  34 us
    another operation x1, local copies, waits for them, and re-layouts, shards(): blocks = dual_ops[0, 0].reshape(4, face_len, 4, face_len)  20.4 us
  transfers between devices with their start and end apart: 56, of which 24 were waited for; matrix products, arithmetic and copies ran while one was open for 5% of the time, Pallas kernels for 0%

commit v1 on v0

--- a/solution.py
+++ b/solution.py
@@ -43,7 +43,14 @@
         return jnp.einsum("gjfi,fki->gkj", blocks, vector, precision=HIGH)
 
     def coarse(coef):
-        gathered = lax.all_gather(coef, "row", axis=1, tiled=True)
+        ways, here = (lax.axis_size("row"), lax.axis_index("row"))
+        gathered, reach = (coef, 1)
+        while reach < ways:
+            theirs = lax.ppermute(gathered, "row", [(d, d ^ reach) for d in range(ways)])
+            mine_first = jnp.concatenate([gathered, theirs], axis=1)
+            theirs_first = jnp.concatenate([theirs, gathered], axis=1)
+            gathered = jnp.where(here & reach == 0, mine_first, theirs_first)
+            reach = 2 * reach
         partial_amps = lax.dot_general(
             gathered,
             coarse_inverse,

time: 944 us -> 945 us (level)
  blocking collectives: 454 us -> 364 us
  starting transfers between devices: 124 us -> 169 us
  waiting for transfers between devices: 40.5 us -> 80.9 us
    all_gather x7 -> x0, blocking collectives: 80.8 us -> none  [coarse(): gathered = lax.all_gather(coef, 'row', axis=1, tiled=True)]
    ppermute x0 -> x21, starting transfers between devices: none -> 43.9 us  [coarse(): lax.ppermute(gathered, 'row', [(d, d ^ reach) for d in range(ways)])]
    ppermute x0 -> x21, waiting for transfers between devices: none -> 38.8 us  [coarse(): lax.ppermute(gathered, 'row', [(d, d ^ reach) for d in range(ways)])]
  transfers between devices with their start and end apart: 56 -> 77, of which waited for: 24 -> 45; matrix products, arithmetic and copies ran while one was open for 5% -> 5% of each run, Pallas kernels for 0% -> 0%
where the time goes in v1:
time: 945 us; the launch traced here: 934 us
  blocking collectives  364 us (39%)
  matrix products  292 us (31%)
  starting transfers between devices  169 us (18%)
  waiting for transfers between devices  80.9 us (9%)
  local copies, waits for them, and re-layouts  21.6 us (2%)
    dot_general x12, matrix products, apply_dual(): return jnp.einsum('gjfi,fki->gkj', blocks, vector, precision=HIGH)  281 us
    psum x6, blocking collectives, shards(): numer_all, denom_all = lax.psum((numer, denom), ('row', 'col'))  241 us
    psum x7, blocking collectives, coarse(): summed = lax.psum(partial_amps, 'col')  123 us
    ppermute x28, starting transfers between devices, padded(): lax.ppermute(lax.slice_in_dim(block, block.shape[dim] - width, None, axis...  87.1 us
    ppermute x21, starting transfers between devices, coarse(): lax.ppermute(gathered, 'row', [(d, d ^ reach) for d in range(ways)])  43.9 us
    ppermute x21, waiting for transfers between devices, coarse(): lax.ppermute(gathered, 'row', [(d, d ^ reach) for d in range(ways)])  38.8 us
    ppermute x28, starting transfers between devices, padded(): lax.ppermute(lax.slice_in_dim(block, 0, width, axis=dim), axis, backward)  37.7 us
    ppermute x28, waiting for transfers between devices, padded(): lax.ppermute(lax.slice_in_dim(block, 0, width, axis=dim), axis, backward)  36.7 us
  transfers between devices with their start and end apart: 77, of which 45 were waited for; matrix products, arithmetic and copies ran while one was open for 5% of the time, Pallas kernels for 0%

profile of v1, /device:TPU:0, one launch (start us, length us, event | category | flops | bytes accessed | tf_op | source)
XLA Modules:
  0.0 933.9 jit_solution(1080999307292843878)
XLA Ops:
  13.2 19.8 %psum.133 = f32[32,256]{1,0:T(8,128)S(1)} all-reduce(f32[32,256]{1,0:T(8,128)S(1)} %fusion.134), channel_id=1, replica_groups=mesh['row'=8,'col'=4] {'col'}, use_global_device_ids=true, to_apply=%region_0.1 | all-reduce | flops 8192 | bytes 65536 | tf_op jit(solution)/shard_map/psum | solution.py:61
  47.1 20.4 %reshape_squeeze.3 = f32[4,512,4,512]{3,2,1,0:T(4,128)} reshape(f32[1,1,2048,2048]{3,2,1,0:T(8,128)} %param.6) | data formatting | bytes 33554432 | tf_op jit(solution)/shard_map/reshape;squeeze | solution.py:32
  74.8 24.6 %fusion.24 = f32[4,32,512]{2,1,0:T(8,128)S(1)} fusion(f32[4,512,4,512]{3,2,1,0:T(4,128)} %reshape_squeeze.3, f32[4,32,512]{2,1,0:T(8,128)S(1)} %convolution_bitcast_fusion.6, f32[1,32,512]{2,1,0:T(8,128)S(1)} %collective-permute-done.6, f32[1,32,512]{2,1,0:T(8,128)S(1)} %collective-permute-done.5, f32[1,32,512]{2,1,0:T(8,128)S(1)} %collective-permute-done.4, ...), kind=kOutput, calls=%fused_computation.24 | convolution fusion | flops 1610874880 | bytes 17563648 | tf_op jit(solution)/shard_map/gjfi,fki->gkj/dot_general | solution.py:43
  157.0 22.3 %fusion.78 = f32[32]{0:T(128)S(1)} fusion(f32[4,32,512]{2,1,0:T(8,128)S(1)} %get-tuple-element.27, f32[4,512,4,512]{3,2,1,0:T(4,128)} %reshape_squeeze.3), kind=kOutput, calls=%fused_computation.49 | convolution fusion | flops 1610743808 | bytes 17039488 | tf_op jit(solution)/shard_map/gjfi,fki->gkj/dot_general | solution.py:43
  179.3 40.4 %all-reduce.5 = (f32[32]{0:T(128)S(1)}, f32[32]{0:T(128)S(1)}) all-reduce(f32[32]{0:T(128)S(1)} %get-tuple-element.26, f32[32]{0:T(128)S(1)} %fusion.78), channel_id=1, replica_groups=mesh['row'=8,'col'=4] {'row','col'}, use_global_device_ids=true, to_apply=%region_3.4 | all-reduce | flops 64 | bytes 512 | tf_op jit(solution)/shard_map/psum | solution.py:81
  219.8 24.6 %fusion.30 = f32[4,32,512]{2,1,0:T(8,128)S(1)} fusion(f32[4,512,4,512]{3,2,1,0:T(4,128)} %reshape_squeeze.3, f32[4,32,512]{2,1,0:T(8,128)S(1)} %maximum_select_fusion.5), kind=kOutput, calls=%fused_computation.26 | convolution fusion | flops 1610612736 | bytes 17301504 | tf_op jit(solution)/shard_map/gjfi,fki->gkj/dot_general | solution.py:43
  269.9 17.4 %psum.137 = f32[32,256]{1,0:T(8,128)S(1)} all-reduce(f32[32,256]{1,0:T(8,128)S(1)} %fusion.146), channel_id=1, replica_groups=mesh['row'=8,'col'=4] {'col'}, use_global_device_ids=true, to_apply=%region_6.7 | all-reduce | flops 8192 | bytes 65536 | tf_op jit(solution)/shard_map/psum | solution.py:61
  299.9 22.3 %fusion.81 = f32[32]{0:T(128)S(1)} fusion(f32[4,32,512]{2,1,0:T(8,128)S(1)} %get-tuple-element.23, f32[4,512,4,512]{3,2,1,0:T(4,128)} %reshape_squeeze.3), kind=kOutput, calls=%fused_computation.50 | convolution fusion | flops 1610743808 | bytes 17039488 | tf_op jit(solution)/shard_map/gjfi,fki->gkj/dot_general | solution.py:43
  322.2 40.2 %all-reduce.4 = (f32[32]{0:T(128)S(1)}, f32[32]{0:T(128)S(1)}) all-reduce(f32[32]{0:T(128)S(1)} %get-tuple-element.22, f32[32]{0:T(128)S(1)} %fusion.81), channel_id=1, replica_groups=mesh['row'=8,'col'=4] {'row','col'}, use_global_device_ids=true, to_apply=%region_8.9 | all-reduce | flops 64 | bytes 512 | tf_op jit(solution)/shard_map/psum | solution.py:81
  362.4 24.4 %fusion.36 = f32[4,32,512]{2,1,0:T(8,128)S(1)} fusion(f32[4,512,4,512]{3,2,1,0:T(4,128)} %reshape_squeeze.3, f32[4,32,512]{2,1,0:T(8,128)S(1)} %maximum_select_fusion.5, f32[4,32,512]{2,1,0:T(8,128)S(1)} %get-tuple-element.23, f32[32]{0:T(128)S(1)} %div.19, pred[4,512]{1,0:T(4,128)(4,1)S(1)} %bitcast_and_fusion), kind=kOutput, calls=%fused_computation.28 | convolution fusion | flops 1610874880 | bytes 17565824 | tf_op jit(solution)/shard_map/gjfi,fki->gkj/dot_general | solution.py:43
  442.3 22.3 %fusion.84 = f32[32]{0:T(128)S(1)} fusion(f32[4,32,512]{2,1,0:T(8,128)S(1)} %get-tuple-element.21, f32[4,512,4,512]{3,2,1,0:T(4,128)} %reshape_squeeze.3), kind=kOutput, calls=%fused_computation.51 | convolution fusion | flops 1610743808 | bytes 17039488 | tf_op jit(solution)/shard_map/gjfi,fki->gkj/dot_general | solution.py:43
  464.6 40.1 %all-reduce.3 = (f32[32]{0:T(128)S(1)}, f32[32]{0:T(128)S(1)}) all-reduce(f32[32]{0:T(128)S(1)} %get-tuple-element.20, f32[32]{0:T(128)S(1)} %fusion.84), channel_id=1, replica_groups=mesh['row'=8,'col'=4] {'row','col'}, use_global_device_ids=true, to_apply=%region_13.14 | all-reduce | flops 64 | bytes 512 | tf_op jit(solution)/shard_map/psum | solution.py:81
  504.9 24.6 %fusion.42 = f32[4,32,512]{2,1,0:T(8,128)S(1)} fusion(f32[4,512,4,512]{3,2,1,0:T(4,128)} %reshape_squeeze.3, f32[4,32,512]{2,1,0:T(8,128)S(1)} %maximum_select_fusion.3), kind=kOutput, calls=%fused_computation.30 | convolution fusion | flops 1610612736 | bytes 17301504 | tf_op jit(solution)/shard_map/gjfi,fki->gkj/dot_general | solution.py:43
  554.9 17.4 %psum.143 = f32[32,256]{1,0:T(8,128)S(1)} all-reduce(f32[32,256]{1,0:T(8,128)S(1)} %fusion.158), channel_id=1, replica_groups=mesh['row'=8,'col'=4] {'col'}, use_global_device_ids=true, to_apply=%region_16.17 | all-reduce | flops 8192 | bytes 65536 | tf_op jit(solution)/shard_map/psum | solution.py:61
  585.0 22.3 %fusion.87 = f32[32]{0:T(128)S(1)} fusion(f32[4,32,512]{2,1,0:T(8,128)S(1)} %get-tuple-element.19, f32[4,512,4,512]{3,2,1,0:T(4,128)} %reshape_squeeze.3), kind=kOutput, calls=%fused_computation.52 | convolution fusion | flops 1610743808 | bytes 17039488 | tf_op jit(solution)/shard_map/gjfi,fki->gkj/dot_general | solution.py:43
  607.3 40.4 %all-reduce.2 = (f32[32]{0:T(128)S(1)}, f32[32]{0:T(128)S(1)}) all-reduce(f32[32]{0:T(128)S(1)} %get-tuple-element.18, f32[32]{0:T(128)S(1)} %fusion.87), channel_id=1, replica_groups=mesh['row'=8,'col'=4] {'row','col'}, use_global_device_ids=true, to_apply=%region_18.19 | all-reduce | flops 64 | bytes 512 | tf_op jit(solution)/shard_map/psum | solution.py:81
  647.7 24.4 %fusion.48 = f32[4,32,512]{2,1,0:T(8,128)S(1)} fusion(f32[4,512,4,512]{3,2,1,0:T(4,128)} %reshape_squeeze.3, f32[4,32,512]{2,1,0:T(8,128)S(1)} %maximum_select_fusion.3, f32[4,32,512]{2,1,0:T(8,128)S(1)} %get-tuple-element.19, f32[32]{0:T(128)S(1)} %div.21, pred[4,512]{1,0:T(4,128)(4,1)S(1)} %bitcast_and_fusion), kind=kOutput, calls=%fused_computation.32 | convolution fusion | flops 1610874880 | bytes 17565824 | tf_op jit(solution)/shard_map/gjfi,fki->gkj/dot_general | solution.py:43
  697.6 17.4 %psum.146 = f32[32,256]{1,0:T(8,128)S(1)} all-reduce(f32[32,256]{1,0:T(8,128)S(1)} %fusion.164), channel_id=1, replica_groups=mesh['row'=8,'col'=4] {'col'}, use_global_device_ids=true, to_apply=%region_21.22 | all-reduce | flops 8192 | bytes 65536 | tf_op jit(solution)/shard_map/psum | solution.py:61
  727.6 22.3 %fusion.90 = f32[32]{0:T(128)S(1)} fusion(f32[4,32,512]{2,1,0:T(8,128)S(1)} %get-tuple-element.17, f32[4,512,4,512]{3,2,1,0:T(4,128)} %reshape_squeeze.3), kind=kOutput, calls=%fused_computation.53 | convolution fusion | flops 1610743808 | bytes 17039488 | tf_op jit(solution)/shard_map/gjfi,fki->gkj/dot_general | solution.py:43
  749.9 40.2 %all-reduce.1 = (f32[32]{0:T(128)S(1)}, f32[32]{0:T(128)S(1)}) all-reduce(f32[32]{0:T(128)S(1)} %get-tuple-element.16, f32[32]{0:T(128)S(1)} %fusion.90), channel_id=1, replica_groups=mesh['row'=8,'col'=4] {'row','col'}, use_global_device_ids=true, to_apply=%region_23.24 | all-reduce | flops 64 | bytes 512 | tf_op jit(solution)/shard_map/psum | solution.py:81
  790.2 24.6 %fusion.54 = f32[4,32,512]{2,1,0:T(8,128)S(1)} fusion(f32[4,512,4,512]{3,2,1,0:T(4,128)} %reshape_squeeze.3, f32[4,32,512]{2,1,0:T(8,128)S(1)} %maximum_select_fusion.1), kind=kOutput, calls=%fused_computation.34 | convolution fusion | flops 1610612736 | bytes 17301504 | tf_op jit(solution)/shard_map/gjfi,fki->gkj/dot_general | solution.py:43
  840.3 17.4 %psum.149 = f32[32,256]{1,0:T(8,128)S(1)} all-reduce(f32[32,256]{1,0:T(8,128)S(1)} %fusion.170), channel_id=1, replica_groups=mesh['row'=8,'col'=4] {'col'}, use_global_device_ids=true, to_apply=%region_26.27 | all-reduce | flops 8192 | bytes 65536 | tf_op jit(solution)/shard_map/psum | solution.py:61
  870.3 22.4 %fusion.93 = f32[32]{0:T(128)S(1)} fusion(f32[4,32,512]{2,1,0:T(8,128)S(1)} %get-tuple-element.15, f32[4,512,4,512]{3,2,1,0:T(4,128)} %reshape_squeeze.3), kind=kOutput, calls=%fused_computation.54 | convolution fusion | flops 1610743808 | bytes 17039488 | tf_op jit(solution)/shard_map/gjfi,fki->gkj/dot_general | solution.py:43
  892.7 39.9 %all-reduce = (f32[32]{0:T(128)S(1)}, f32[32]{0:T(128)S(1)}) all-reduce(f32[32]{0:T(128)S(1)} %get-tuple-element.14, f32[32]{0:T(128)S(1)} %fusion.93), channel_id=1, replica_groups=mesh['row'=8,'col'=4] {'row','col'}, use_global_device_ids=true, to_apply=%region_28.29 | all-reduce | flops 64 | bytes 512 | tf_op jit(solution)/shard_map/psum | solution.py:81
  (239 shorter events, 300.0 us)
Async XLA Ops:
  33.5 34.0 %collective-permute-start.3 = (f32[1,32,512]{2,1,0:T(8,128)S(1)}, f32[1,32,512]{2,1,0:T(8,128)S(1)}, u32[]{:S(2)}, u32[]{:S(2)}) collective-permute-start(f32[1,32,512]{2,1,0:T(8,128)S(1)} %get-tuple-element.82), channel_id=1, source_target_pairs={{0,4},{4,8},{8,12},{12,16},{16,20},{20,24},{24,28},{1,5},{5,9},{9,... | collective-permute-start | bytes 196616 | tf_op jit(solution)/shard_map/ppermute | solution.py:16
  34.8 34.2 %collective-permute-start.6 = (f32[1,32,512]{2,1,0:T(8,128)S(1)}, f32[1,32,512]{2,1,0:T(8,128)S(1)}, u32[]{:S(2)}, u32[]{:S(2)}) collective-permute-start(f32[1,32,512]{2,1,0:T(8,128)S(1)} %get-tuple-element.83), channel_id=1, source_target_pairs={{1,0},{2,1},{3,2},{5,4},{6,5},{7,6},{9,8},{10,9},{11,10},{13,12},{... | collective-permute-start | bytes 196616 | tf_op jit(solution)/shard_map/ppermute | solution.py:19
  36.1 34.2 %collective-permute-start.5 = (f32[1,32,512]{2,1,0:T(8,128)S(1)}, f32[1,32,512]{2,1,0:T(8,128)S(1)}, u32[]{:S(2)}, u32[]{:S(2)}) collective-permute-start(f32[1,32,512]{2,1,0:T(8,128)S(1)} %get-tuple-element.84), channel_id=1, source_target_pairs={{0,1},{1,2},{2,3},{4,5},{5,6},{6,7},{8,9},{9,10},{10,11},{12,13},{... | collective-permute-start | bytes 196616 | tf_op jit(solution)/shard_map/ppermute | solution.py:16
  40.6 34.2 %collective-permute-start.4 = (f32[1,32,512]{2,1,0:T(8,128)S(1)}, f32[1,32,512]{2,1,0:T(8,128)S(1)}, u32[]{:S(2)}, u32[]{:S(2)}) collective-permute-start(f32[1,32,512]{2,1,0:T(8,128)S(1)} %get-tuple-element.85), channel_id=1, source_target_pairs={{4,0},{8,4},{12,8},{16,12},{20,16},{24,20},{28,24},{5,1},{9,5},{13... | collective-permute-start | bytes 196616 | tf_op jit(solution)/shard_map/ppermute | solution.py:19
  42.9 60.3 %collective-permute-start.11 = (f32[1,32,512]{2,1,0:T(8,128)S(1)}, f32[1,32,512]{2,1,0:T(8,128)S(1)}, u32[]{:S(2)}, u32[]{:S(2)}) collective-permute-start(f32[1,32,512]{2,1,0:T(8,128)S(1)} %get-tuple-element.74), channel_id=1, source_target_pairs={{0,4},{4,8},{8,12},{12,16},{16,20},{20,24},{24,28},{1,5},{5,9},{9,... | collective-permute-start | bytes 196616 | tf_op jit(solution)/shard_map/ppermute | solution.py:16
  67.5 37.0 %collective-permute-start.12 = (f32[1,32,512]{2,1,0:T(8,128)S(1)}, f32[1,32,512]{2,1,0:T(8,128)S(1)}, u32[]{:S(2)}, u32[]{:S(2)}) collective-permute-start(f32[1,32,512]{2,1,0:T(8,128)S(1)} %get-tuple-element.75), channel_id=1, source_target_pairs={{4,0},{8,4},{12,8},{16,12},{20,16},{24,20},{28,24},{5,1},{9,5},{13... | collective-permute-start | bytes 196616 | tf_op jit(solution)/shard_map/ppermute | solution.py:19
  68.9 40.1 %collective-permute-start.14 = (f32[1,32,512]{2,1,0:T(8,128)S(1)}, f32[1,32,512]{2,1,0:T(8,128)S(1)}, u32[]{:S(2)}, u32[]{:S(2)}) collective-permute-start(f32[1,32,512]{2,1,0:T(8,128)S(1)} %get-tuple-element.76), channel_id=1, source_target_pairs={{1,0},{2,1},{3,2},{5,4},{6,5},{7,6},{9,8},{10,9},{11,10},{13,12},{... | collective-permute-start | bytes 196616 | tf_op jit(solution)/shard_map/ppermute | solution.py:19
  70.3 40.3 %collective-permute-start.13 = (f32[1,32,512]{2,1,0:T(8,128)S(1)}, f32[1,32,512]{2,1,0:T(8,128)S(1)}, u32[]{:S(2)}, u32[]{:S(2)}) collective-permute-start(f32[1,32,512]{2,1,0:T(8,128)S(1)} %get-tuple-element.77), channel_id=1, source_target_pairs={{0,1},{1,2},{2,3},{4,5},{5,6},{6,7},{8,9},{9,10},{10,11},{12,13},{... | collective-permute-start | bytes 196616 | tf_op jit(solution)/shard_map/ppermute | solution.py:16
  99.5 11.1 %collective-permute-start.7 = (f32[1,32,512]{2,1,0:T(8,128)S(1)}, f32[1,32,512]{2,1,0:T(8,128)S(1)}, u32[]{:S(2)}, u32[]{:S(2)}) collective-permute-start(f32[1,32,512]{2,1,0:T(8,128)S(1)} %get-tuple-element.78), channel_id=1, source_target_pairs={{0,4},{4,8},{8,12},{12,16},{16,20},{20,24},{24,28},{1,5},{5,9},{9,... | collective-permute-start | bytes 196616 | tf_op jit(solution)/shard_map/ppermute | solution.py:16
  103.2 7.4 collective-permute-start.10
  144.8 8.5 collective-permute-start.18
  244.4 8.5 collective-permute-start.22
  287.7 8.6 collective-permute-start.29
  386.8 8.5 collective-permute-start.33
  430.1 8.9 collective-permute-start.40
  431.4 7.6 collective-permute-start.43
  529.5 8.5 collective-permute-start.44
  572.8 8.7 collective-permute-start.51
  574.1 7.4 collective-permute-start.54
  672.1 8.5 collective-permute-start.55
  715.4 8.6 collective-permute-start.62
  814.8 8.5 collective-permute-start.66
  858.1 8.7 collective-permute-start.73
  859.4 7.4 collective-permute-start.76
  (58 other events, 536.3 us)
